TPU v7x, 32 devices: a whole 2x2x4 slice. The times are simulated.
32 devices in a mesh: chan: 4 (over x, core), az: 2 (over y), rng: 4 (over z).
Axes of the slice: x: 2, y: 2, z: 4, core: 2. Of those that a mesh axis runs over, the one named last changes fastest.
Arguments:
- raw: float32 [2, 16, 64, 16384], P(None, 'chan', 'rng', 'az'), may hold values from -6 to 6
- taps: float32 [2, 17, 64], P(None, None, 'rng'), may hold values from -1.5 to 1.5
- recon: float32 [2, 16, 16, 16384], P(None, 'az', None, ('chan', 'rng')), may hold values from -1 to 1
- channel_slot: int32 [16], replicated, may hold values from 0 to 15, each once
Outputs:
- reconstructed: float32 [2, 16, 4, 16, 16384], P(None, None, None, 'az', ('chan', 'rng'))
Inputs may be any that keep to these rules, and one draw needn't show every extreme that they name: `channel_slot`: a permutation of the channels.
All inputs are finite; a program needn't handle non-finite values.
Results may differ from a plain program's by a relative error of at most 0.0003.
Values sent between devices are 32-bit elements; how exact they have to be, the bound alone decides.
No kernel may reach another device: no remote copies, remote signals or barrier semaphores. Data moves between devices by JAX's collectives and lax.ppermute only.
A program may use at most 192 MiB of HBM per device.

v0:
```python
import math

import jax
import jax.numpy as jnp
from jax import lax
from jax.sharding import PartitionSpec as P


def with_halo(shard, sides, width):
    for axis, dim in sides:
        size, length = (lax.axis_size(axis), shard.shape[dim])
        up = [(i, (i + 1) % size) for i in range(size - 1)]
        down = [(j, i) for i, j in up]
        last = lax.slice_in_dim(shard, length - width, length, axis=dim)
        leading = lax.slice_in_dim(shard, 0, width, axis=dim)
        before = lax.ppermute(last, axis, up)
        after = lax.ppermute(leading, axis, down)
        shard = jnp.concatenate([before, shard, after], axis=dim)
    return shard


def phases(first, second, length):
    left = jnp.arange(first, dtype=jnp.int32)
    right = jnp.arange(second, dtype=jnp.int32)
    product = left[:, None] * right[None, :] % length
    angle = product.astype(jnp.float32) * (2.0 * math.pi / length)
    return (jnp.cos(angle), jnp.sin(angle))


def azimuth_fft(block):
    count = block.shape[-1]
    rows = math.isqrt(count)
    while count % rows:
        rows = rows - 1
    cols = count // rows
    lead = block.shape[1:-1]
    high = lax.Precision.HIGHEST
    real_in = block[0].reshape(lead + (rows, cols))
    imag_in = block[1].reshape(lead + (rows, cols))
    cosine_first, sine_first = phases(rows, rows, rows)
    first_real = jnp.einsum("...ab,af->...bf", real_in, cosine_first, precision=high) + jnp.einsum(
        "...ab,af->...bf", imag_in, sine_first, precision=high
    )
    first_imag = jnp.einsum("...ab,af->...bf", imag_in, cosine_first, precision=high) - jnp.einsum(
        "...ab,af->...bf", real_in, sine_first, precision=high
    )
    twist_cos, twist_sin = phases(cols, rows, count)
    turned_real = first_real * twist_cos + first_imag * twist_sin
    turned_imag = first_imag * twist_cos - first_real * twist_sin
    cosine_second, sine_second = phases(cols, cols, cols)
    out_real = jnp.einsum(
        "...bf,bg->...gf", turned_real, cosine_second, precision=high
    ) + jnp.einsum("...bf,bg->...gf", turned_imag, sine_second, precision=high)
    out_imag = jnp.einsum(
        "...bf,bg->...gf", turned_imag, cosine_second, precision=high
    ) - jnp.einsum("...bf,bg->...gf", turned_real, sine_second, precision=high)
    scale = 1.0 / math.sqrt(count)
    return jnp.stack([out_real.reshape(lead + (count,)), out_imag.reshape(lead + (count,))]) * scale


def shards(raw, taps, recon, channel_slot):
    width = taps.shape[1]
    half = (width - 1) // 2
    strip_rows = raw.shape[2]
    padded = with_halo(raw, (("rng", 2),), half)
    real_part = jnp.zeros(raw.shape[1:], jnp.float32)
    imag_part = jnp.zeros(raw.shape[1:], jnp.float32)
    for offset in range(width):
        seg_real = padded[0, :, offset : offset + strip_rows, :]
        seg_imag = padded[1, :, offset : offset + strip_rows, :]
        tap_real = taps[0, offset][None, :, None]
        tap_imag = taps[1, offset][None, :, None]
        real_part = real_part + tap_real * seg_real - tap_imag * seg_imag
        imag_part = imag_part + tap_real * seg_imag + tap_imag * seg_real
    filtered = jnp.stack([real_part, imag_part])
    spectrum = azimuth_fft(lax.all_to_all(filtered, "az", split_axis=2, concat_axis=3, tiled=True))
    strips = lax.axis_size("rng")
    groups = lax.axis_size("chan")
    local_channels = spectrum.shape[1]
    local_range = spectrum.shape[2]
    moved = lax.all_to_all(
        spectrum[:, None], ("chan", "rng"), split_axis=4, concat_axis=1, tiled=True
    )
    bins = moved.shape[-1]
    moved = moved.reshape((2, groups, strips, local_channels, local_range, bins))
    doppler = jnp.transpose(moved, (0, 1, 3, 2, 4, 5)).reshape(
        (2, groups * local_channels, strips * local_range, bins)
    )
    channels = doppler.shape[1]
    selector = (channel_slot[:, None] == jnp.arange(channels, dtype=jnp.int32)[None, :]).astype(
        jnp.float32
    )
    piece = lax.all_gather(recon, "az", axis=1, tiled=True)
    arranged = jnp.einsum("pkjf,cj->pkcf", piece, selector, precision=lax.Precision.HIGHEST)
    shape = (piece.shape[1], doppler.shape[2], doppler.shape[3])
    out_real = jnp.zeros(shape, jnp.float32)
    out_imag = jnp.zeros(shape, jnp.float32)
    for channel in range(channels):
        mat_real = arranged[0, :, channel, None, :]
        mat_imag = arranged[1, :, channel, None, :]
        data_real = doppler[0, channel][None]
        data_imag = doppler[1, channel][None]
        out_real = out_real + mat_real * data_real - mat_imag * data_imag
        out_imag = out_imag + mat_real * data_imag + mat_imag * data_real
    result = jnp.stack([out_real, out_imag])
    total_range = result.shape[2]
    return result.reshape((2, result.shape[1], strips, total_range // strips, result.shape[3]))


def solution(mesh):
    return jax.shard_map(
        shards,
        mesh=mesh,
        in_specs=(
            P(None, "chan", "rng", "az"),
            P(None, None, "rng"),
            P(None, "az", None, ("chan", "rng")),
            P(),
        ),
        out_specs=P(None, None, None, "az", ("chan", "rng")),
        check_vma=False,
    )
```

profile of v0, /device:TPU:0, one launch (start us, length us, event | category | flops | bytes accessed | tf_op | source)
XLA Modules:
  0.0 701.4 jit_solution(1237962557530691339)
XLA Ops:
  6.5 2.5 fusion.71
  9.0 5.1 collective-permute-start
  14.1 1.3 collective-permute-start.1
  15.4 0.0 copy-done.7
  15.5 0.5 slice_reduce_fusion.33
  15.9 0.4 slice_reduce_fusion.32
  16.4 0.0 copy-start
  16.4 42.5 %collective-permute-done = f32[2,4,8,8192]{3,2,1,0:T(8,128)S(1)} collective-permute-done((f32[2,4,8,8192]{3,2,1,0:T(8,128)S(1)}, f32[2,4,8,8192]{3,2,1,0:T(8,128)S(1)}, u32[]{:S(2)}, u32[]{:S(2)}) %collective-permute-start) | collective-permute-done | bytes 2097184 | tf_op jit(solution)/shard_map/ppermute | solution.py:16
  58.9 1.5 constant_dynamic-update-slice_fusion.1
  60.4 4.2 constant_dynamic-update-slice_fusion
  64.6 0.0 collective-permute-done.1
  64.6 1.5 constant_dynamic-update-slice_fusion.2
  66.1 44.7 %multiply_subtract_fusion.2 = f32[1,4,16,8192]{3,2,1,0:T(8,128)} fusion(f32[2,4,24,8192]{3,2,1,0:T(8,128)} %constant_dynamic-update-slice_fusion.2, f32[2,4,24,8192]{3,2,1,0:T(8,128)} %get-tuple-element.73, f32[2,4,16,8192]{3,2,1,0:T(8,128)S(1)} %copy-done, f32[16]{0:T(128)S(1)} %get-tuple-element.37, f32[16]{0:T(128)S(1)} %get-tuple-element.38, ...), kind=kLoop, calls=%fused_computation.11 | loop fusion | flops 35127296 | bytes 73402496 | tf_op jit(solution)/shard_map/sub | solution.py:73
  110.8 44.8 %multiply_add_fusion.2 = f32[1,4,16,8192]{3,2,1,0:T(8,128)} fusion(f32[2,4,24,8192]{3,2,1,0:T(8,128)} %constant_dynamic-update-slice_fusion.2, f32[2,4,24,8192]{3,2,1,0:T(8,128)} %get-tuple-element.73, f32[2,4,16,8192]{3,2,1,0:T(8,128)S(1)} %copy-done, f32[16]{0:T(128)S(1)} %get-tuple-element.37, f32[16]{0:T(128)S(1)} %get-tuple-element.38, ...), kind=kLoop, calls=%fused_computation.10 | loop fusion | flops 35127296 | bytes 73402496 | tf_op jit(solution)/shard_map/add | solution.py:74
  155.5 2.5 pad_maximum_fusion
  158.1 4.7 copy.126
  162.8 6.1 all-to-all-start
  168.9 0.3 fusion.24
  169.1 0.1 copy.132
  169.2 0.3 fusion.23
  169.5 0.1 copy.137
  169.6 46.1 %all-to-all-done = f32[2,4,16,8192]{3,1,0,2:T(4,128)} async-done(((f32[2,4,16,8192]{3,1,0,2:T(4,128)}), f32[2,4,16,8192]{3,1,0,2:T(4,128)}, u32[]{:S(2)}, u32[]{:S(2)}) %all-to-all-start) | async-done | bytes 4194336 | tf_op jit(solution)/shard_map/all_to_all | solution.py:76
  215.7 5.4 copy.224
  221.1 2.3 fusion.70
  223.3 3.1 reshape_squeeze.7
  226.4 4.9 fusion.6
  231.3 0.0 copy-done.2
  231.3 4.2 reshape_squeeze.6
  235.5 0.0 copy-start.4
  235.5 0.0 copy-start.5
  235.5 5.4 fusion.8
  240.9 0.0 copy-done.4
  240.9 0.0 copy-done.5
  240.9 0.0 copy-start.3
  240.9 3.7 convolution_subtract_fusion
  244.6 3.6 convolution_add_fusion
  248.2 0.0 copy-start.1
  248.2 2.5 fusion
  250.7 3.5 fusion.1
  254.2 3.7 add_bitcast_fusion
  257.9 2.7 stack.18
  260.6 5.8 subtract_bitcast_fusion
  266.4 2.9 stack.19
  269.3 3.9 maximum_multiply_fusion
  273.2 44.6 %copy.138 = f32[2,1,4,8,16384]{3,2,1,0,4:T(4,128)} copy(f32[2,1,4,8,16384]{4,3,2,1,0:T(8,128)} %maximum_multiply_fusion) | data formatting | bytes 8388608 | tf_op jit(solution)/shard_map/mul | solution.py:58
  317.8 82.8 %reshape.729 = f32[16,1,65536]{2,1,0:T(1,128)} reshape(f32[16384,2,1,4,8]{4,3,2,1,0:T(4,128)} %bitcast.180) | data formatting | bytes 8388608
  400.5 7.0 all-to-all-start.1
  407.5 0.0 all-gather.2.cloned.1.call-start
  407.6 0.7 all-gather.2.cloned.1.call-update
  408.3 35.1 %all-gather.2.cloned.1.call-done = f32[2,16,16,1024]{3,2,1,0:T(8,128)} async-done(((f32[2,8,16,1024]{3,2,1,0:T(8,128)}), f32[2,16,16,1024]{3,2,1,0:T(8,128)}) %all-gather.2.cloned.1.call-update) | async-done | bytes 2097168 | tf_op jit(solution)/shard_map/all_gather | solution.py:93
  443.4 2.7 convolution_bitcast_fusion
  446.1 1.1 fusion.72
  447.5 0.8 fusion.73
  448.5 53.3 %all-to-all-done.1 = f32[16,1,65536]{2,1,0:T(1,128)} async-done(((f32[16,1,65536]{2,1,0:T(1,128)}), f32[16,1,65536]{2,1,0:T(1,128)}, u32[]{:S(2)}, u32[]{:S(2)}) %all-to-all-start.1) | async-done | bytes 4194336 | tf_op jit(solution)/shard_map/all_to_all | solution.py:81
  501.8 0.5 broadcast.1262
  502.4 13.7 %reduce.68 = f32[16,65536]{1,0:T(8,128)} reduce(f32[16,1,65536]{2,1,0:T(1,128)} %all-to-all-done.1, f32[]{:T(128)} %broadcast.1262), dimensions={1}, to_apply=%all_to_all.25.reduce_sub_computation | reduce | bytes 8388612 | tf_op jit(solution)/shard_map/all_to_all | solution.py:81
  516.1 108.8 %reshape.730 = f32[16384,2,1,4,8]{4,3,2,1,0:T(4,128)} reshape(f32[16,65536]{1,0:T(8,128)} %reduce.68) | data formatting | bytes 8388608
  624.9 53.3 %copy.158 = f32[2,1,4,8,16,1024]{5,3,2,4,0,1:T(8,128)} copy(f32[2,1,4,8,16,1024]{3,2,0,5,4,1:T(4,128)} %bitcast.17) | data formatting | bytes 8388608 | tf_op jit(solution)/shard_map/all_to_all | solution.py:81
  678.2 2.5 copy.141
  680.7 0.2 slice_bitcast_fusion.31
  680.9 0.2 slice_bitcast_fusion.30
  681.1 5.3 multiply_subtract_fusion
  686.5 5.3 multiply_add_fusion
  691.8 2.3 pad_maximum_fusion.1
  (25 shorter events, 0.4 us)
Async XLA Ops:
  6.5 8.9 %copy-start.7 = (f32[2,17,16]{1,2,0:T(8,128)S(1)}, f32[2,17,16]{1,2,0:T(8,128)}, u32[]{:S(2)}) copy-start(f32[2,17,16]{1,2,0:T(8,128)} %param.5) | copy-start | bytes 6532
  9.0 49.8 %collective-permute-start = (f32[2,4,8,8192]{3,2,1,0:T(8,128)S(1)}, f32[2,4,8,8192]{3,2,1,0:T(8,128)S(1)}, u32[]{:S(2)}, u32[]{:S(2)}) collective-permute-start(f32[2,4,8,8192]{3,2,1,0:T(8,128)S(1)} %get-tuple-element.75), channel_id=1, source_target_pairs={{0,1},{1,2},{2,3},{4,5},{5,6},{6,7},{8,9},{9,10},{10,11},{12,13},{... | collective-permute-start | bytes 6291464 | tf_op jit(solution)/shard_map/ppermute | solution.py:16
  14.1 50.5 %collective-permute-start.1 = (f32[2,4,8,8192]{3,2,1,0:T(8,128)S(1)}, f32[2,4,8,8192]{3,2,1,0:T(8,128)S(1)}, u32[]{:S(2)}, u32[]{:S(2)}) collective-permute-start(f32[2,4,8,8192]{3,2,1,0:T(8,128)S(1)} %get-tuple-element.76), channel_id=1, source_target_pairs={{1,0},{2,1},{3,2},{5,4},{6,5},{7,6},{9,8},{10,9},{11,10},{13,12},{... | collective-permute-start | bytes 6291464 | tf_op jit(solution)/shard_map/ppermute | solution.py:17
  16.4 44.0 %copy-start = (f32[2,4,16,8192]{3,2,1,0:T(8,128)S(1)}, f32[2,4,16,8192]{3,2,1,0:T(8,128)}, u32[]{:S(2)}) copy-start(f32[2,4,16,8192]{3,2,1,0:T(8,128)} %param.4) | copy-start | bytes 12582916
  162.8 52.9 %all-to-all-start = ((f32[2,4,16,8192]{3,1,0,2:T(4,128)}), f32[2,4,16,8192]{3,1,0,2:T(4,128)}, u32[]{:S(2)}, u32[]{:S(2)}) async-start(f32[2,4,16,8192]{3,1,0,2:T(4,128)} %copy.126), calls=%async_computation | async-start | bytes 8388608 | tf_op jit(solution)/shard_map/all_to_all | solution.py:76
  226.4 4.9 copy-start.2
  235.5 5.4 copy-start.4
  235.5 5.4 copy-start.5
  240.9 3.7 copy-start.3
  248.2 6.0 copy-start.1
  266.4 2.9 copy-start.6
  400.5 42.8 %copy-start.8 = (s32[16]{0:T(128)S(1)}, s32[16]{0:T(128)}, u32[]{:S(2)}) copy-start(s32[16]{0:T(128)} %param.7) | copy-start | bytes 196
  400.5 101.3 %all-to-all-start.1 = ((f32[16,1,65536]{2,1,0:T(1,128)}), f32[16,1,65536]{2,1,0:T(1,128)}, u32[]{:S(2)}, u32[]{:S(2)}) async-start(f32[16,1,65536]{2,1,0:T(1,128)} %reshape.729), calls=%async_computation.1 | async-start | bytes 8388608 | tf_op jit(solution)/shard_map/all_to_all | solution.py:81
  407.5 35.8 %all-gather.2.cloned.1.call-start = ((), (), s32[]{:S(2)}) async-start(), calls=%async_computation.2 | async-start | bytes 3145728 | tf_op jit(solution)/shard_map/all_gather | solution.py:93
Sparse Core Ops, SparseCore 0:
  409.9 33.4 all-gather.1
where the time goes:
time: 715 us; the launch traced here: 701 us
  local copies, waits for them, and re-layouts  331 us (46%)
  waiting for transfers between devices  178 us (25%)
  other arithmetic  123 us (17%)
  matrix products  35.7 us (5%)
  starting transfers between devices  19.5 us (3%)
  between operations  14.2 us (2%)
    unnamed x37, local copies, waits for them, and re-layouts  194 us
    all_to_all x2, local copies, waits for them, and re-layouts, shards(): lax.all_to_all(spectrum[:, None], ('chan', 'rng'), split_axis=4, concat_a...  53.9 us
    all_to_all x1, waiting for transfers between devices, shards(): lax.all_to_all(spectrum[:, None], ('chan', 'rng'), split_axis=4, concat_a...  53.3 us
    all_to_all x1, waiting for transfers between devices, shards(): lax.all_to_all(filtered, 'az', split_axis=2, concat_axis=3, tiled=True)  46.1 us
    add x1, other arithmetic, shards(): imag_part = imag_part + tap_real * seg_imag + tap_imag * seg_real  44.8 us
    sub x1, other arithmetic, shards(): real_part = real_part + tap_real * seg_real - tap_imag * seg_imag  44.7 us
    mul x1, local copies, waits for them, and re-layouts, azimuth_fft(): jnp.stack([out_real.reshape(lead + (count,)), out_imag.reshape(lead + (co...  44.6 us
    ppermute x1, waiting for transfers between devices, with_halo(): before = lax.ppermute(last, axis, up)  42.5 us
  transfers between devices with their start and end apart: 5, of which 4 were waited for; matrix products, arithmetic and copies ran while one was open for 2% of the time, Pallas kernels for 0%

commit v1 on v0

--- a/solution.py
+++ b/solution.py
@@ -2,8 +2,284 @@
 
 import jax
 import jax.numpy as jnp
+import ml_dtypes
+import numpy as np
 from jax import lax
+from jax.experimental import pallas as pl
+from jax.experimental.pallas import tpu as pltpu
 from jax.sharding import PartitionSpec as P
+
+LANES = 128
+SUB = 8
+
+
+def ring(size, step):
+    return [(i, (i + step) % size) for i in range(size)]
+
+
+def split_three(matrix):
+    high = matrix.astype(np.float32).astype(ml_dtypes.bfloat16)
+    low = (matrix - high.astype(np.float64)).astype(ml_dtypes.bfloat16)
+    return np.concatenate([high, high, low], axis=1)
+
+
+def two_parts(value):
+    high = value.astype(jnp.bfloat16)
+    return high, (value - high.astype(jnp.float32)).astype(jnp.bfloat16)
+
+
+def fft_tables(slow, count, azs):
+    own = slow // azs
+    h = np.arange(slow)
+    place = np.concatenate([(-i * own + np.arange(own)) % slow for i in range(azs)])
+    angle = 2 * np.pi * ((h[:, None] * place[None, :]) % slow) / slow
+    first = np.block([[np.cos(angle), np.sin(angle)], [-np.sin(angle), np.cos(angle)]])
+    b = np.arange(LANES)
+    tables = []
+    for me in range(azs):
+        turn = 2 * np.pi * ((h[:, None] * (b[None, :] + me * own * LANES)) % count) / count
+        tables.append(np.stack([np.cos(turn), -np.sin(turn)]))
+    m = np.arange(count // slow)
+    angle = 2 * np.pi * ((m[:, None] * b[None, :]) % LANES) / LANES
+    second = np.block([[np.cos(angle), np.sin(angle)], [-np.sin(angle), np.cos(angle)]])
+    second = second / math.sqrt(count)
+    return split_three(first), np.stack(tables).astype(np.float32), split_three(second)
+
+
+def fft_kernel(azs, own, peers, rows, *refs):
+    inputs = refs[1 : 1 + azs]
+    first_ref, turn_ref, second_ref, out_ref, scratch = refs[1 + azs :]
+    slow = own * azs
+    subs = LANES // peers
+    for tile in range(rows // SUB):
+        for part in range(2):
+            for i in range(azs):
+                for a in range(own):
+                    scratch[pl.ds(part * slow + i * own + a, SUB, stride=2 * slow), :] = inputs[i][
+                        part, 0, tile * SUB : (tile + 1) * SUB, a * LANES : (a + 1) * LANES
+                    ]
+        for row in range(0, SUB, 2):
+            x = jnp.concatenate(
+                [scratch[(row + e) * 2 * slow : (row + e + 1) * 2 * slow, :] for e in range(2)], axis=1
+            )
+            high, low = two_parts(x)
+            y = jnp.dot(
+                first_ref[...],
+                jnp.concatenate([high, low, high], axis=0),
+                preferred_element_type=jnp.float32,
+            )
+            turned = []
+            for e in range(2):
+                real = y[:slow, e * LANES : (e + 1) * LANES]
+                imag = y[slow:, e * LANES : (e + 1) * LANES]
+                turned.append(
+                    jnp.concatenate(
+                        [
+                            real * turn_ref[0, 0] - imag * turn_ref[0, 1],
+                            real * turn_ref[0, 1] + imag * turn_ref[0, 0],
+                        ],
+                        axis=1,
+                    )
+                )
+            high, low = two_parts(jnp.concatenate(turned, axis=0))
+            z = lax.dot_general(
+                second_ref[...],
+                jnp.concatenate([high, low, high], axis=1),
+                (((1,), (1,)), ((), ())),
+                preferred_element_type=jnp.float32,
+            )
+            for part in range(2):
+                for peer in range(peers):
+                    for e in range(2):
+                        out_ref[peer, part, tile, pl.ds(row + e, subs, stride=SUB), :] = z[
+                            part * LANES + peer * subs : part * LANES + (peer + 1) * subs,
+                            e * slow : (e + 1) * slow,
+                        ]
+
+
+def fft_call(index, raw, received, tables, peers, per, chunk, rows):
+    azs = 1 + len(received)
+    own = raw.shape[3] // LANES
+    slow = own * azs
+    subs = LANES // peers
+    first, turn, second = tables
+    row_at, row_count = rows
+    grid = (row_count // SUB,)
+    spec = pltpu.PrefetchScalarGridSpec(
+        num_scalar_prefetch=1,
+        grid=grid,
+        in_specs=[
+            pl.BlockSpec(
+                (2, 1, SUB, own * LANES), lambda g, ix: (0, ix[0] * per + chunk, g + row_at // SUB, 0)
+            )
+        ]
+        + [pl.BlockSpec((2, 1, SUB, own * LANES), lambda g, ix: (0, 0, g, 0))] * len(received)
+        + [
+            pl.BlockSpec(first.shape, lambda g, ix: (0, 0)),
+            pl.BlockSpec((1, 2, slow, LANES), lambda g, ix: (ix[0], 0, 0, 0)),
+            pl.BlockSpec(second.shape, lambda g, ix: (0, 0)),
+        ],
+        out_specs=pl.BlockSpec((peers, 2, 1, SUB * subs, LANES), lambda g, ix: (0, 0, g, 0, 0)),
+        scratch_shapes=[pltpu.VMEM((SUB * 2 * slow, LANES), jnp.float32)],
+    )
+    out = jax.ShapeDtypeStruct((peers, 2, row_count // SUB, SUB * subs, LANES), jnp.float32)
+    work = row_count * own * azs * LANES
+    return pl.pallas_call(
+        lambda *refs: fft_kernel(azs, own, peers, SUB, *refs),
+        grid_spec=spec,
+        out_shape=out,
+        name="azimuth",
+        cost_estimate=pl.CostEstimate(flops=work * 2 * 8 * 128 * 3, bytes_accessed=work * 16, transcendentals=0),
+    )(index, raw, *received, first, turn, second)
+
+
+def band_matrix(taps, me, azs):
+    width, total = taps.shape[1:]
+    half = (width - 1) // 2
+    strips_rows = total
+    at = jnp.arange(strips_rows, dtype=jnp.int32)
+    tap = at[None, :] - at[:, None] + half
+    hit = tap[:, :, None] == jnp.arange(width, dtype=jnp.int32)
+    table = jnp.transpose(taps, (0, 2, 1))
+    band = jnp.sum(jnp.where(hit[None], table[:, :, None, :], 0.0), axis=3)
+    real = jnp.concatenate([band[0], -band[1]], axis=1)
+    imag = jnp.concatenate([band[1], band[0]], axis=1)
+    return jnp.stack([real, imag])
+
+
+def filter_kernel(azs, chans, strips, tiles, subs, w_ref, *refs):
+    ins, outs = refs[: len(tiles)], refs[len(tiles) :]
+    w = w_ref[...]
+    columns = w.shape[1] // 3
+    rounded = w.astype(jnp.bfloat16).astype(jnp.float32)
+    low_part = lax.broadcasted_iota(jnp.int32, w.shape, 1) >= 2 * columns
+    weights = jnp.where(low_part, w - rounded, rounded).astype(jnp.bfloat16)
+    step = 4
+    for sub_at in range(0, subs, step):
+        blocks = []
+        for part in range(2):
+            for strip in range(strips):
+                for ref, count in zip(ins, tiles):
+                    for tile in range(count):
+                        blocks.append(
+                            jnp.concatenate(
+                                [
+                                    ref[strip, part, tile, (sub_at + s) * SUB : (sub_at + s + 1) * SUB, :]
+                                    for s in range(step)
+                                ],
+                                axis=1,
+                            )
+                        )
+        high, low = two_parts(jnp.concatenate(blocks, axis=0))
+        y = jnp.dot(
+            weights, jnp.concatenate([high, low, high], axis=0), preferred_element_type=jnp.float32
+        )
+        at = 0
+        for i in range(azs):
+            for part in range(2):
+                for strip in range(strips):
+                    for s in range(step):
+                        outs[i][part, 0, strip, sub_at + s, :, :] = y[
+                            at : at + SUB, s * LANES : (s + 1) * LANES
+                        ]
+                    at += SUB
+
+
+def filter_call(weights, pieces, chans, azs, subs):
+    peers = pieces[0].shape[0]
+    strips = peers // chans
+    tiles = [p.shape[2] for p in pieces]
+    out = jax.ShapeDtypeStruct((2, chans, strips, subs, SUB, LANES), jnp.float32)
+    return pl.pallas_call(
+        lambda *refs: filter_kernel(azs, chans, strips, tiles, subs, *refs),
+        grid=(chans,),
+        in_specs=[pl.BlockSpec(weights.shape, lambda g: (0, 0))]
+        + [pl.BlockSpec((strips,) + p.shape[1:], lambda g: (g, 0, 0, 0, 0)) for p in pieces],
+        out_specs=[pl.BlockSpec((2, 1, strips, subs, SUB, LANES), lambda g: (0, g, 0, 0, 0, 0))] * azs,
+        out_shape=[out] * azs,
+        name="range_filter",
+        cost_estimate=pl.CostEstimate(
+            flops=2 * weights.shape[0] * weights.shape[1] * chans * subs * LANES,
+            bytes_accessed=8 * sum(math.prod(p.shape) for p in pieces),
+            transcendentals=0,
+        ),
+    )(weights, *pieces)
+
+
+def mix_kernel(azs, chans, local, per, chunk, kept, index_ref, slot_ref, *refs):
+    data, mats = refs[:azs], refs[azs : 2 * azs]
+    prior = refs[2 * azs] if kept else None
+    out_ref = refs[-1]
+    me = index_ref[0]
+    strips = data[0].shape[2]
+    here = mats[0].shape[1]
+    pair = 2 if here % 2 == 0 else 1
+    for j in range(azs):
+        base = lax.rem(me - j + azs, azs) * here
+
+        def body(step, _, j=j, base=base):
+            totals = [[[None, None] for _ in range(strips)] for _ in range(pair)]
+            if kept:
+                for e in range(pair):
+                    for s in range(strips):
+                        for p in range(2):
+                            totals[e][s][p] = prior[p, base + step * pair + e, s]
+            for i in range(azs):
+                source = lax.rem(me - i + azs, azs)
+                for chan in range(chans):
+                    slot = slot_ref[chan * local + source * per + chunk]
+                    values = [(data[i][0, chan, s, 0], data[i][1, chan, s, 0]) for s in range(strips)]
+                    for e in range(pair):
+                        row = step * pair + e
+                        ar = jnp.broadcast_to(mats[j][0, row, pl.ds(slot, 1), :], (SUB, LANES))
+                        ai = jnp.broadcast_to(mats[j][1, row, pl.ds(slot, 1), :], (SUB, LANES))
+                        for s, (dr, di) in enumerate(values):
+                            real = ar * dr - ai * di
+                            imag = ar * di + ai * dr
+                            old = totals[e][s]
+                            totals[e][s] = [
+                                real if old[0] is None else old[0] + real,
+                                imag if old[1] is None else old[1] + imag,
+                            ]
+            for e in range(pair):
+                for s in range(strips):
+                    for p in range(2):
+                        out_ref[p, base + step * pair + e, s] = totals[e][s][p]
+            return 0
+
+        lax.fori_loop(0, here // pair, body, 0)
+
+
+def mix_call(index, slots, data, mats, prior, chans, local, per, chunk):
+    azs = len(data)
+    _, _, strips, subs, _, _ = data[0].shape
+    here, width = mats[0].shape[1:3]
+    total = here * azs
+    out = jax.ShapeDtypeStruct((2, total, strips, SUB, subs * LANES), jnp.float32)
+    out_spec = pl.BlockSpec((2, total, strips, SUB, LANES), lambda g, ix, sl: (0, 0, 0, 0, g))
+    kept = prior is not None
+    return pl.pallas_call(
+        lambda *refs: mix_kernel(azs, chans, local, per, chunk, kept, *refs),
+        grid_spec=pltpu.PrefetchScalarGridSpec(
+            num_scalar_prefetch=2,
+            grid=(subs,),
+            in_specs=[
+                pl.BlockSpec((2, chans, strips, 1, SUB, LANES), lambda g, ix, sl: (0, 0, 0, g, 0, 0))
+            ]
+            * azs
+            + [pl.BlockSpec((2, here, width, LANES), lambda g, ix, sl: (0, 0, 0, g))] * azs
+            + [out_spec] * kept,
+            out_specs=out_spec,
+        ),
+        out_shape=out,
+        name="reconstruct",
+        input_output_aliases={2 + 2 * azs: 0} if kept else {},
+        cost_estimate=pl.CostEstimate(
+            flops=8 * total * strips * SUB * subs * LANES * chans * azs,
+            bytes_accessed=4 * (2 * total * strips * SUB * subs * LANES) * (2 if kept else 1),
+            transcendentals=0,
+        ),
+    )(index, slots, *data, *mats, *([prior] if kept else []))
 
 
 def with_halo(shard, sides, width):
@@ -58,7 +334,7 @@
     return jnp.stack([out_real.reshape(lead + (count,)), out_imag.reshape(lead + (count,))]) * scale
 
 
-def shards(raw, taps, recon, channel_slot):
+def general_shards(raw, taps, recon, channel_slot):
     width = taps.shape[1]
     half = (width - 1) // 2
     strip_rows = raw.shape[2]
@@ -107,6 +383,50 @@
     return result.reshape((2, result.shape[1], strips, total_range // strips, result.shape[3]))
 
 
+def shards(raw, taps, recon, channel_slot):
+    chans, azs, strips = (lax.axis_size(n) for n in ("chan", "az", "rng"))
+    _, local, rows, pulses = raw.shape
+    fits = local % azs == 0 and rows == azs * SUB and pulses * azs == LANES * LANES
+    if not (fits and LANES % (chans * strips) == 0):
+        return general_shards(raw, taps, recon, channel_slot)
+    me = lax.axis_index("az").astype(jnp.int32)
+    index = me[None]
+    per = local // azs
+    count = pulses * azs
+    peers = chans * strips
+    slow = count // LANES
+    subs = LANES // peers
+    tables = [jnp.asarray(t) for t in fft_tables(slow, count, azs)]
+
+    def give(step, chunk):
+        to = lax.rem(me + step, azs)
+        block = lax.dynamic_slice(raw, (0, to * per + chunk, 0, 0), (2, 1, rows, pulses))
+        return lax.ppermute(block, "az", ring(azs, step))
+
+    received = [[give(i, j) for i in range(1, azs)] for j in range(per)]
+    mats = [recon] + [lax.ppermute(recon, "az", ring(azs, i)) for i in range(1, azs)]
+
+    copies = jnp.broadcast_to(taps[None], (strips,) + taps.shape)
+    all_taps = lax.all_to_all(copies, "rng", 0, 0, tiled=True)
+    all_taps = jnp.transpose(all_taps, (1, 2, 0, 3)).reshape(2, taps.shape[1], strips * rows)
+    band = band_matrix(all_taps, me, azs)
+    band = band.reshape(2, strips, azs, SUB, 2 * strips * rows)
+    band = jnp.transpose(band, (2, 0, 1, 3, 4)).reshape(azs, -1, 2 * strips * rows)
+    band = lax.dynamic_slice_in_dim(jnp.concatenate([band, band]), me, azs, 0)
+    weights = jnp.tile(band.reshape(-1, 2 * strips * rows), (1, 3))
+
+    result = None
+    for j in range(per):
+        spectrum = fft_call(index, raw, received[j], tables, peers, per, j, (0, rows))
+        moved = lax.all_to_all(spectrum, ("chan", "rng"), 0, 0, tiled=True)
+        filtered = filter_call(weights, [moved], chans, azs, subs)
+        data = [filtered[0]] + [
+            lax.ppermute(filtered[i], "az", ring(azs, i)) for i in range(1, azs)
+        ]
+        result = mix_call(index, channel_slot, data, mats, result, chans, local, per, j)
+    return result
+
+
 def solution(mesh):
     return jax.shard_map(
         shards,

time: 715 us -> 187 us (0.26); the launches traced: 701 us -> 186 us
  local copies, waits for them, and re-layouts: 331 us -> 7.82 us
  other arithmetic: 123 us -> 1.16 us
  waiting for transfers between devices: 178 us -> 111 us
  Pallas kernels: 0 us -> 41.8 us
  matrix products: 35.7 us -> 0 us
  between operations: 14.2 us -> 0.16 us
    unnamed x37 -> x15, local copies, waits for them, and re-layouts: 194 us -> 4.44 us
    all_to_all x3 -> x1, local copies, waits for them, and re-layouts: 59.3 us -> 0.52 us  [shards(): all_taps = lax.all_to_all(copies, 'rng', 0, 0, tiled=True)]
    add x2 -> x1, other arithmetic: 50.1 us -> 0.01 us  [band_matrix(): tap = at[None, :] - at[:, None] + half]
    sub x2 -> x0, other arithmetic: 50 us -> none  [the longest x1 44.7 us: shards(): real_part = real_part + tap_real * seg_real - tap_imag * seg_imag]
    mul x3 -> x0, local copies, waits for them, and re-layouts: 45 us -> none  [the longest x1 44.6 us: azimuth_fft(): jnp.stack([out_real.reshape(lead + (count,)), out_imag.reshape(lead + (co...]
    all_to_all x2 -> x3, waiting for transfers between devices: 99.4 us -> 57.2 us  [the longest x2 57.2 us: shards(): moved = lax.all_to_all(spectrum, ('chan', 'rng'), 0, 0, tiled=True)]
    pallas_call x0 -> x6, Pallas kernels: none -> 41.8 us  [the longest x2 20.4 us: mix_call(): pl.pallas_call(lambda *refs: mix_kernel(azs, chans, local, per, chunk, ke...]
    dot_general x9 -> x0, matrix products: 35.7 us -> none  [the longest x1 5.76 us: azimuth_fft(): jnp.einsum('...bf,bg->...gf', turned_real, sine_second, precision=high)]
  transfers between devices with their start and end apart: 5 -> 8, of which waited for: 4 -> 5; matrix products, arithmetic and copies ran while one was open for 2% -> 2% of each run, Pallas kernels for 0% -> 17%
where the time goes in v1:
time: 187 us; the launch traced here: 186 us
  waiting for transfers between devices  111 us (59%)
  Pallas kernels  41.8 us (22%)
  starting transfers between devices  23.7 us (13%)
  local copies, waits for them, and re-layouts  7.82 us (4%)
    all_to_all x2, waiting for transfers between devices, shards(): moved = lax.all_to_all(spectrum, ('chan', 'rng'), 0, 0, tiled=True)  57.2 us
    ppermute x2, waiting for transfers between devices, give(): return lax.ppermute(block, 'az', ring(azs, step))  41.6 us
    pallas_call x2, Pallas kernels, mix_call(): pl.pallas_call(lambda *refs: mix_kernel(azs, chans, local, per, chunk, ke...  20.4 us
    pallas_call x2, Pallas kernels, fft_call(): pl.pallas_call(lambda *refs: fft_kernel(azs, own, peers, SUB, *refs), gri...  12.6 us
    ppermute x2, waiting for transfers between devices, shards(): lax.ppermute(filtered[i], 'az', ring(azs, i))  12.5 us
    all_to_all x2, starting transfers between devices, shards(): moved = lax.all_to_all(spectrum, ('chan', 'rng'), 0, 0, tiled=True)  10.6 us
    pallas_call x2, Pallas kernels, filter_call(): pl.pallas_call(lambda *refs: filter_kernel(azs, chans, strips, tiles, sub...  8.76 us
    all_to_all x1, starting transfers between devices, shards(): all_taps = lax.all_to_all(copies, 'rng', 0, 0, tiled=True)  4.87 us
  transfers between devices with their start and end apart: 8, of which 5 were waited for; matrix products, arithmetic and copies ran while one was open for 2% of the time, Pallas kernels for 17%

profile of v1, /device:TPU:0, one launch (start us, length us, event | category | flops | bytes accessed | tf_op | source)
XLA Modules:
  0.0 186.0 jit_solution(17007384459273574992)
XLA Ops:
  0.0 0.0 copy-start
  0.0 1.7 constant_dynamic-slice_fusion
  1.7 3.1 %collective-permute-start.3 = (f32[2,1,16,8192]{3,2,1,0:T(8,128)S(1)}, f32[2,1,16,8192]{3,2,1,0:T(8,128)S(1)}, u32[]{:S(2)}, u32[]{:S(2)}) collective-permute-start(f32[2,1,16,8192]{3,2,1,0:T(8,128)S(1)} %get-tuple-element.13), channel_id=1, source_target_pairs={{0,4},{4,0},{1,5},{5,1},{2,6},{6,2},{3,7},{7,3},{8,12},{12,8},{9,1... | collective-permute-start | bytes 3145736 | tf_op jit(solution)/shard_map/ppermute | solution.py:404
  4.8 0.0 copy-done
  4.8 0.7 reshape.49
  5.5 4.9 %all-to-all-start = ((f32[4,1,544]{2,1,0:T(1,128)}), f32[4,1,544]{2,1,0:T(1,128)S(1)}, u32[]{:S(2)}, u32[]{:S(2)}) async-start(f32[4,1,544]{2,1,0:T(1,128)} %reshape.49), calls=%async_computation | async-start | bytes 20480 | tf_op jit(solution)/shard_map/all_to_all | solution.py:410
  10.4 17.6 %collective-permute-done.3.refs_2_ = f32[2,1,16,8192]{3,2,1,0:T(8,128)S(1)} collective-permute-done((f32[2,1,16,8192]{3,2,1,0:T(8,128)S(1)}, f32[2,1,16,8192]{3,2,1,0:T(8,128)S(1)}, u32[]{:S(2)}, u32[]{:S(2)}) %collective-permute-start.3) | collective-permute-done | bytes 1048608 | tf_op jit(solution)/shard_map/ppermute | solution.py:404
  27.9 0.0 copy-start.5
  27.9 1.0 copy-done.5
  28.9 6.3 %azimuth.3 = f32[16,2,2,64,128]{4,3,2,1,0:T(8,128)} custom-call(s32[1]{0:T(128)} %bitcast.refs_0_, f32[2,4,16,8192]{3,2,1,0:T(8,128)} %refs_1_.5, f32[2,1,16,8192]{3,2,1,0:T(8,128)} %copy-done.5, bf16[256,768]{1,0:T(8,128)(2,1)} %constant.28.clone.refs_3_, f32[2,2,128,128]{3,2,1,0:T(8,128)} %constant.29.clone.refs_4_, bf16[256,768]{1,0:T(8,128)(2,1)} %constant.30.clone.refs_5_), custom_call_target="tpu_custom_call" | custom-call | flops 1610612736 | bytes 4194304 | tf_op jit(solution)/shard_map/azimuth/pallas_call | solution.py:127
  35.2 0.0 all-to-all-done
  35.2 6.1 %all-to-all-start.2 = ((f32[16,2,2,64,128]{4,3,2,1,0:T(8,128)}), f32[16,2,2,64,128]{4,3,2,1,0:T(8,128)S(1)}, u32[]{:S(2)}, u32[]{:S(2)}) async-start(f32[16,2,2,64,128]{4,3,2,1,0:T(8,128)} %azimuth.3), calls=%async_computation.2 | async-start | bytes 4194304 | tf_op jit(solution)/shard_map/all_to_all | solution.py:421
  41.4 1.6 collective-permute-start
  43.0 24.0 %collective-permute-done.refs_2_ = f32[2,1,16,8192]{3,2,1,0:T(8,128)} collective-permute-done((f32[2,1,16,8192]{3,2,1,0:T(8,128)S(1)}, f32[2,1,16,8192]{3,2,1,0:T(8,128)}, u32[]{:S(2)}, u32[]{:S(2)}) %collective-permute-start) | collective-permute-done | bytes 1048608 | tf_op jit(solution)/shard_map/ppermute | solution.py:404
  67.0 6.3 %azimuth.2 = f32[16,2,2,64,128]{4,3,2,1,0:T(8,128)} custom-call(s32[1]{0:T(128)} %bitcast.refs_0_, f32[2,4,16,8192]{3,2,1,0:T(8,128)} %refs_1_.5, f32[2,1,16,8192]{3,2,1,0:T(8,128)} %collective-permute-done.refs_2_, bf16[256,768]{1,0:T(8,128)(2,1)} %constant.28.clone.refs_3_, f32[2,2,128,128]{3,2,1,0:T(8,128)} %constant.29.clone.refs_4_, ...), custom_call_target="tpu_custom_call" | custom-call | flops 1610612736 | bytes 4194304 | tf_op jit(solution)/shard_map/azimuth/pallas_call | solution.py:127
  73.3 0.0 copy-start.2
  73.3 17.4 %all-to-all-done.2.refs_1_ = f32[16,2,2,64,128]{4,3,2,1,0:T(8,128)S(1)} async-done(((f32[16,2,2,64,128]{4,3,2,1,0:T(8,128)}), f32[16,2,2,64,128]{4,3,2,1,0:T(8,128)S(1)}, u32[]{:S(2)}, u32[]{:S(2)}) %all-to-all-start.2) | async-done | bytes 2097184 | tf_op jit(solution)/shard_map/all_to_all | solution.py:421
  90.7 0.0 copy-start.1
  90.7 1.3 copy-done.1
  92.0 4.4 %all-to-all-start.1 = ((f32[16,2,2,64,128]{4,3,2,1,0:T(8,128)}), f32[16,2,2,64,128]{4,3,2,1,0:T(8,128)}, u32[]{:S(2)}, u32[]{:S(2)}) async-start(f32[16,2,2,64,128]{4,3,2,1,0:T(8,128)} %azimuth.2), calls=%async_computation.1 | async-start | bytes 4194304 | tf_op jit(solution)/shard_map/all_to_all | solution.py:421
  96.5 0.0 copy-done.2
  96.5 1.6 collective-permute-start.2
  98.1 0.1 iota_compare_fusion
  98.1 0.5 broadcast.19
  98.7 0.6 reduce
  99.3 0.1 reshape.50
  99.4 0.1 copy.25
  99.5 0.1 reshape.47
  99.7 0.4 select_reduce_fusion
  100.0 0.1 maximum_bitcast_fusion
  100.2 0.1 copy.28
  100.3 0.8 copy.29.refs_0_
  101.1 4.4 %range_filter.3 = (f32[2,4,4,8,8,128]{5,4,3,2,1,0:T(8,128)}, f32[2,4,4,8,8,128]{5,4,3,2,1,0:T(8,128)}) custom-call(f32[128,384]{1,0:T(8,128)} %copy.29.refs_0_, f32[16,2,2,64,128]{4,3,2,1,0:T(8,128)} %copy-done.1), custom_call_target="tpu_custom_call" | custom-call | flops 402653184 | bytes 4194304 | tf_op jit(solution)/shard_map/range_filter/pallas_call | solution.py:193
  105.5 0.5 collective-permute-start.4
  106.0 39.8 %all-to-all-done.1.refs_1_ = f32[16,2,2,64,128]{4,3,2,1,0:T(8,128)} async-done(((f32[16,2,2,64,128]{4,3,2,1,0:T(8,128)}), f32[16,2,2,64,128]{4,3,2,1,0:T(8,128)}, u32[]{:S(2)}, u32[]{:S(2)}) %all-to-all-start.1) | async-done | bytes 2097184 | tf_op jit(solution)/shard_map/all_to_all | solution.py:421
  145.8 4.4 %range_filter.2 = (f32[2,4,4,8,8,128]{5,4,3,2,1,0:T(8,128)}, f32[2,4,4,8,8,128]{5,4,3,2,1,0:T(8,128)}) custom-call(f32[128,384]{1,0:T(8,128)} %copy.29.refs_0_, f32[16,2,2,64,128]{4,3,2,1,0:T(8,128)} %all-to-all-done.1.refs_1_), custom_call_target="tpu_custom_call" | custom-call | flops 402653184 | bytes 4194304 | tf_op jit(solution)/shard_map/range_filter/pallas_call | solution.py:193
  150.2 1.5 collective-permute-start.1
  151.7 0.0 collective-permute-done.2.refs_5_
  151.7 0.0 copy-start.3
  151.7 0.0 collective-permute-done.4.refs_3_
  151.7 0.0 copy-start.4
  151.7 1.0 copy-done.3
  152.7 0.3 copy-done.4
  153.0 9.7 %reconstruct.2.refs_6_ = f32[2,16,4,8,1024]{4,3,2,1,0:T(8,128)} custom-call(s32[1]{0:T(128)} %bitcast.refs_0_, s32[16]{0:T(128)} %refs_1_.7, f32[2,4,4,8,8,128]{5,4,3,2,1,0:T(8,128)} %get-tuple-element.11.refs_2_, f32[2,4,4,8,8,128]{5,4,3,2,1,0:T(8,128)} %copy-done.4, f32[2,8,16,1024]{3,2,1,0:T(8,128)} %refs_4_.5, f32[2,8,16,1024]{3,2,1,0:T(8,128)} %copy-done.3), custom_call_target="tpu_custom_call" | custom-call | flops 33554432 | bytes 4194304 | tf_op jit(solution)/shard_map/reconstruct/pallas_call | solution.py:261
  162.8 12.5 %collective-permute-done.1.refs_3_ = f32[2,4,4,8,8,128]{5,4,3,2,1,0:T(8,128)} collective-permute-done((f32[2,4,4,8,8,128]{5,4,3,2,1,0:T(8,128)}, f32[2,4,4,8,8,128]{5,4,3,2,1,0:T(8,128)}, u32[]{:S(2)}, u32[]{:S(2)}) %collective-permute-start.1) | collective-permute-done | bytes 1048608 | tf_op jit(solution)/shard_map/ppermute | solution.py:424
  175.3 10.7 %reconstruct.3 = f32[2,16,4,8,1024]{4,3,2,1,0:T(8,128)} custom-call(s32[1]{0:T(128)} %bitcast.refs_0_, s32[16]{0:T(128)} %refs_1_.7, f32[2,4,4,8,8,128]{5,4,3,2,1,0:T(8,128)} %get-tuple-element.9.refs_2_, f32[2,4,4,8,8,128]{5,4,3,2,1,0:T(8,128)} %collective-permute-done.1.refs_3_, f32[2,8,16,1024]{3,2,1,0:T(8,128)} %refs_4_.5, ...), custom_call_target="tpu_custom_call", output_to_operand_aliasing={{}: (6, {})} | custom-call | flops 33554432 | bytes 8388608 | tf_op jit(solution)/shard_map/reconstruct/pallas_call | solution.py:261
  (9 shorter events, 0.1 us)
Async XLA Ops:
  0.0 4.8 %copy-start = (f32[2,17,16]{1,2,0:T(8,128)S(1)}, f32[2,17,16]{1,2,0:T(8,128)}, u32[]{:S(2)}) copy-start(f32[2,17,16]{1,2,0:T(8,128)} %param.8) | copy-start | bytes 6532
  1.7 26.2 %collective-permute-start.3 = (f32[2,1,16,8192]{3,2,1,0:T(8,128)S(1)}, f32[2,1,16,8192]{3,2,1,0:T(8,128)S(1)}, u32[]{:S(2)}, u32[]{:S(2)}) collective-permute-start(f32[2,1,16,8192]{3,2,1,0:T(8,128)S(1)} %get-tuple-element.13), channel_id=1, source_target_pairs={{0,4},{4,0},{1,5},{5,1},{2,6},{6,2},{3,7},{7,3},{8,12},{12,8},{9,1... | collective-permute-start | bytes 3145736 | tf_op jit(solution)/shard_map/ppermute | solution.py:404
  5.5 29.7 %all-to-all-start = ((f32[4,1,544]{2,1,0:T(1,128)}), f32[4,1,544]{2,1,0:T(1,128)S(1)}, u32[]{:S(2)}, u32[]{:S(2)}) async-start(f32[4,1,544]{2,1,0:T(1,128)} %reshape.49), calls=%async_computation | async-start | bytes 20480 | tf_op jit(solution)/shard_map/all_to_all | solution.py:410
  27.9 1.0 copy-start.5
  35.2 55.4 %all-to-all-start.2 = ((f32[16,2,2,64,128]{4,3,2,1,0:T(8,128)}), f32[16,2,2,64,128]{4,3,2,1,0:T(8,128)S(1)}, u32[]{:S(2)}, u32[]{:S(2)}) async-start(f32[16,2,2,64,128]{4,3,2,1,0:T(8,128)} %azimuth.3), calls=%async_computation.2 | async-start | bytes 4194304 | tf_op jit(solution)/shard_map/all_to_all | solution.py:421
  41.4 25.6 %collective-permute-start = (f32[2,1,16,8192]{3,2,1,0:T(8,128)S(1)}, f32[2,1,16,8192]{3,2,1,0:T(8,128)}, u32[]{:S(2)}, u32[]{:S(2)}) collective-permute-start(f32[2,1,16,8192]{3,2,1,0:T(8,128)S(1)} %get-tuple-element.14), channel_id=1, source_target_pairs={{0,4},{4,0},{1,5},{5,1},{2,6},{6,2},{3,7},{7,3},{8,12},{12,8},{9,1... | collective-permute-start | bytes 3145736 | tf_op jit(solution)/shard_map/ppermute | solution.py:404
  73.3 23.2 %copy-start.2 = (f32[2,8,16,1024]{3,2,1,0:T(8,128)S(1)}, f32[2,8,16,1024]{3,2,1,0:T(8,128)}, u32[]{:S(2)}) copy-start(f32[2,8,16,1024]{3,2,1,0:T(8,128)} %refs_4_.5) | copy-start | bytes 3145732
  90.7 1.3 copy-start.1
  92.0 53.8 %all-to-all-start.1 = ((f32[16,2,2,64,128]{4,3,2,1,0:T(8,128)}), f32[16,2,2,64,128]{4,3,2,1,0:T(8,128)}, u32[]{:S(2)}, u32[]{:S(2)}) async-start(f32[16,2,2,64,128]{4,3,2,1,0:T(8,128)} %azimuth.2), calls=%async_computation.1 | async-start | bytes 4194304 | tf_op jit(solution)/shard_map/all_to_all | solution.py:421
  96.5 55.2 %collective-permute-start.2 = (f32[2,8,16,1024]{3,2,1,0:T(8,128)S(1)}, f32[2,8,16,1024]{3,2,1,0:T(8,128)S(1)}, u32[]{:S(2)}, u32[]{:S(2)}) collective-permute-start(f32[2,8,16,1024]{3,2,1,0:T(8,128)S(1)} %copy-done.2), channel_id=1, source_target_pairs={{0,4},{4,0},{1,5},{5,1},{2,6},{6,2},{3,7},{7,3},{8,12},{12,8},{9,1... | collective-permute-start | bytes 3145736 | tf_op jit(solution)/shard_map/ppermute | solution.py:407
  105.5 46.2 %collective-permute-start.4 = (f32[2,4,4,8,8,128]{5,4,3,2,1,0:T(8,128)}, f32[2,4,4,8,8,128]{5,4,3,2,1,0:T(8,128)S(1)}, u32[]{:S(2)}, u32[]{:S(2)}) collective-permute-start(f32[2,4,4,8,8,128]{5,4,3,2,1,0:T(8,128)} %get-tuple-element.12), channel_id=1, source_target_pairs={{0,4},{4,0},{1,5},{5,1},{2,6},{6,2},{3,7},{7,3},{8,12},{12,8},{9,1... | collective-permute-start | bytes 3145736 | tf_op jit(solution)/shard_map/ppermute | solution.py:424
  150.2 25.1 %collective-permute-start.1 = (f32[2,4,4,8,8,128]{5,4,3,2,1,0:T(8,128)}, f32[2,4,4,8,8,128]{5,4,3,2,1,0:T(8,128)}, u32[]{:S(2)}, u32[]{:S(2)}) collective-permute-start(f32[2,4,4,8,8,128]{5,4,3,2,1,0:T(8,128)} %get-tuple-element.10), channel_id=1, source_target_pairs={{0,4},{4,0},{1,5},{5,1},{2,6},{6,2},{3,7},{7,3},{8,12},{12,8},{9,1... | collective-permute-start | bytes 3145736 | tf_op jit(solution)/shard_map/ppermute | solution.py:424
  151.7 1.0 copy-start.3
  151.7 1.3 copy-start.4
